TPU v7x, 32 devices: a whole 2x2x4 slice. The times are simulated.
32 devices in a mesh: tm: 4 (over x, core), space: 8 (over z, y).
Axes of the slice: x: 2, y: 2, z: 4, core: 2. Of those that a mesh axis runs over, the one named last changes fastest.
Arguments:
- frames_in: bfloat16 [24, 64, 128, 128], P('tm', 'space'), may hold values from -6 to 6
- boundary: bfloat16 [5, 2, 128, 128], replicated, may hold values from -6 to 6
- conv_first: bfloat16 [3, 3, 128, 128], replicated, may hold values from -0.1875 to 0.1875
- conv_second: bfloat16 [3, 3, 128, 128], replicated, may hold values from -0.1875 to 0.1875
- norm_gain: float32 [128], replicated, may hold values from 0.1 to 1.9
- qkv_weight: bfloat16 [128, 384], replicated, as said below
- out_weight: bfloat16 [128, 128], replicated, may hold values from -0.5 to 0.5
Outputs:
- block_out: bfloat16 [24, 64, 128, 128], P('tm', 'space')
Inputs may be any that keep to these rules, and one draw needn't show every extreme that they name: `qkv_weight`: a projection matrix.
All inputs are finite; a program needn't handle non-finite values.
Results may differ from a plain program's by a relative error of at most 0.034.
The roundings to bfloat16 on the way count: a program that leaves them out, or rounds other values in their place, can miss the bound.
Values may be sent and summed in bfloat16 or wider, within the bound.
A program may use at most 128 MiB of HBM per device.

v0:
```python
import jax
import jax.numpy as jnp
from jax import lax
from jax.experimental import pallas as pl
from jax.experimental.pallas import tpu as pltpu
from jax.sharding import PartitionSpec as P

HEADS = 8
FRAMES = 24
COARSE = 5


def padded_2(cells, sides, width):
    for axis, dim in sides:
        count = lax.axis_size(axis)
        ends = count - 1
        head = lax.slice_in_dim(cells, 0, width, axis=dim)
        tail = lax.slice_in_dim(cells, cells.shape[dim] - width, cells.shape[dim], axis=dim)
        cells = jnp.concatenate(
            [
                lax.ppermute(tail, axis, [(i, (i + 1) % count) for i in range(ends)]),
                cells,
                lax.ppermute(head, axis, [((i + 1) % count, i) for i in range(ends)]),
            ],
            axis=dim,
        )
    return cells


def interp_matrix(times):
    scaled = times * (COARSE - 1)
    lower = scaled // (FRAMES - 1)
    upper = jnp.minimum(lower + 1, COARSE - 1)
    frac = (scaled - lower * (FRAMES - 1)).astype(jnp.float32) / float(FRAMES - 1)
    levels = jnp.arange(COARSE, dtype=jnp.int32)
    low_hot = (levels[None, :] == lower[:, None]).astype(jnp.float32)
    up_hot = (levels[None, :] == upper[:, None]).astype(jnp.float32)
    return (1.0 - frac)[:, None] * low_hot + frac[:, None] * up_hot


def fix_edges(padded, strips):
    place = lax.axis_index("space")
    last = lax.axis_size("space") - 1
    top_row = jnp.where(place == 0, strips[:, 0:1], padded[:, 0:1])
    bottom_row = jnp.where(place == last, strips[:, 1:2], padded[:, -1:])
    rows = jnp.concatenate([top_row, padded[:, 1:-1], bottom_row], axis=1)
    return jnp.pad(rows, ((0, 0), (0, 0), (1, 1), (0, 0)))


def conv_tile(padded, kernel):
    nframes = padded.shape[0]
    rows = padded.shape[1] - 2
    width = padded.shape[2] - 2
    chans = padded.shape[3]
    total = jnp.zeros((nframes * rows * width, kernel.shape[3]), jnp.float32)
    for shift_r in range(3):
        for shift_c in range(3):
            piece = padded[:, shift_r : shift_r + rows, shift_c : shift_c + width].reshape(
                nframes * rows * width, chans
            )
            total = total + jnp.dot(
                piece, kernel[shift_r, shift_c], preferred_element_type=jnp.float32
            )
    return total.reshape(nframes, rows, width, kernel.shape[3])


def attend_pixels(x, qkv_weight, norm_gain, out_weight, mask, heads_of):
    nframes, group, chans = x.shape
    rows = nframes * group
    head_dim = chans // HEADS
    x = x.reshape(rows, chans)
    mean_sq = jnp.mean(x * x, axis=-1, keepdims=True)
    normed = (x * lax.rsqrt(mean_sq + 1e-06) * norm_gain).astype(jnp.bfloat16)
    qkv = jnp.dot(normed, qkv_weight, preferred_element_type=jnp.float32).astype(jnp.bfloat16)
    query = qkv[:, :chans] * jnp.bfloat16(1.0 / head_dim**0.5)
    key_part = qkv[:, chans : 2 * chans]
    value = qkv[:, 2 * chans :]
    with_ones = jnp.concatenate([value, jnp.ones_like(value)], axis=1)
    num = jnp.zeros((rows, chans), jnp.float32)
    den = jnp.ones((rows, chans), jnp.float32)
    for head in range(HEADS):
        own = heads_of == head
        picked = jnp.where(own, query, jnp.zeros_like(query))
        scores = lax.dot_general(
            picked, key_part, (((1,), (1,)), ((), ())), preferred_element_type=jnp.float32
        )
        scores = scores + mask
        top = jnp.max(scores, axis=-1, keepdims=True)
        expd = jnp.exp(scores - top).astype(jnp.bfloat16)
        both = jnp.dot(expd, with_ones, preferred_element_type=jnp.float32)
        num = jnp.where(own, both[:, :chans], num)
        den = jnp.where(own, both[:, chans:], den)
    attended = (num / den).astype(jnp.bfloat16)
    out = x + jnp.dot(attended, out_weight, preferred_element_type=jnp.float32)
    return out.reshape(nframes, group, chans)


def temporal_kernel(x_ref, gain_ref, qkv_ref, outw_ref, o_ref, mask_ref):
    nframes, pixels, chans = x_ref.shape
    rows = nframes * 8
    row = lax.broadcasted_iota(jnp.int32, (rows, rows), 0)
    col = lax.broadcasted_iota(jnp.int32, (rows, rows), 1)
    mask_ref[...] = jnp.where(lax.rem(row, 8) == lax.rem(col, 8), 0.0, -1e30)
    heads_of = lax.broadcasted_iota(jnp.int32, (rows, chans), 1) // (chans // HEADS)

    def step(i, carry):
        start = pl.multiple_of(i * 16, 16)
        x = x_ref[:, pl.ds(start, 16), :].astype(jnp.float32)
        halves = [
            attend_pixels(
                x[:, k * 8 : k * 8 + 8], qkv_ref[...], gain_ref[...], outw_ref[...],
                mask_ref[...], heads_of,
            )
            for k in range(2)
        ]
        o_ref[:, pl.ds(start, 16), :] = jnp.concatenate(halves, axis=1).astype(o_ref.dtype)
        return carry

    lax.fori_loop(0, pixels // 16, step, 0)


def temporal(resid, norm_gain, qkv_weight, out_weight):
    nframes, pixels, chans = resid.shape
    vmem = pl.BlockSpec(memory_space=pltpu.VMEM)
    return pl.pallas_call(
        temporal_kernel,
        out_shape=jax.ShapeDtypeStruct(resid.shape, resid.dtype),
        in_specs=[vmem] * 4,
        out_specs=vmem,
        scratch_shapes=[pltpu.VMEM((nframes * 8, nframes * 8), jnp.float32)],
        name="temporal",
    )(resid, norm_gain.reshape(1, chans), qkv_weight, out_weight)


def on_device(frames_in, boundary, conv_first, conv_second, norm_gain, qkv_weight, out_weight):
    local_frames = frames_in.shape[0]
    chans = frames_in.shape[3]
    times = lax.axis_index("tm") * local_frames + jnp.arange(local_frames, dtype=jnp.int32)
    weights = interp_matrix(times)
    strips = jnp.einsum("tk,kscx->tscx", weights, boundary.astype(jnp.float32)).astype(jnp.bfloat16)
    padded_in = padded_2(frames_in, (("space", 1),), 1)
    first = conv_tile(fix_edges(padded_in, strips), conv_first)
    hidden = jax.nn.silu(first).astype(jnp.bfloat16)
    padded_hidden = padded_2(hidden, (("space", 1),), 1)
    second = conv_tile(fix_edges(padded_hidden, strips), conv_second)
    resid = (frames_in.astype(jnp.float32) + second).astype(jnp.bfloat16)
    regrouped = lax.all_to_all(resid, "tm", split_axis=1, concat_axis=0, tiled=True)
    layout = regrouped.shape
    mixed = temporal(regrouped.reshape(FRAMES, -1, chans), norm_gain, qkv_weight, out_weight)
    return lax.all_to_all(
        mixed.reshape(layout), "tm", split_axis=0, concat_axis=1, tiled=True
    )


def solution(mesh):
    placed = (P("tm", "space", None, None), P(), P(), P(), P(), P(), P())
    return jax.shard_map(
        on_device,
        mesh=mesh,
        in_specs=placed,
        out_specs=P("tm", "space", None, None),
        check_vma=False,
    )
```

profile of v0, /device:TPU:17, one launch (start us, length us, event | category | flops | bytes accessed | tf_op | source)
XLA Modules:
  0.0 147.9 jit_solution(8717325429562590924)
XLA Ops:
  0.0 1.1 fusion.71
  1.3 3.2 %collective-permute-start.1 = (bf16[6,1,128,128]{3,0,2,1:T(8,128)(2,1)S(1)}, bf16[6,1,128,128]{3,0,2,1:T(8,128)(2,1)S(1)}, u32[]{:S(2)}, u32[]{:S(2)}) collective-permute-start(bf16[6,1,128,128]{3,0,2,1:T(8,128)(2,1)S(1)} %copy.59), channel_id=1, source_target_pairs={{1,0},{2,1},{3,2},{4,3},{5,4},{6,5},{7,6},{9,8},{10,9},{11,10},{12... | collective-permute-start | bytes 589832 | tf_op jit(solution)/shard_map/ppermute | solution.py:23
  4.6 2.2 %collective-permute-start = (bf16[6,1,128,128]{3,0,2,1:T(8,128)(2,1)S(1)}, bf16[6,1,128,128]{3,0,2,1:T(8,128)(2,1)S(1)}, u32[]{:S(2)}, u32[]{:S(2)}) collective-permute-start(bf16[6,1,128,128]{3,0,2,1:T(8,128)(2,1)S(1)} %copy.58), channel_id=1, source_target_pairs={{0,1},{1,2},{2,3},{3,4},{4,5},{5,6},{6,7},{8,9},{9,10},{10,11},{11... | collective-permute-start | bytes 589832 | tf_op jit(solution)/shard_map/ppermute | solution.py:21
  7.3 8.8 %collective-permute-done.1 = bf16[6,1,128,128]{3,0,2,1:T(8,128)(2,1)S(1)} collective-permute-done((bf16[6,1,128,128]{3,0,2,1:T(8,128)(2,1)S(1)}, bf16[6,1,128,128]{3,0,2,1:T(8,128)(2,1)S(1)}, u32[]{:S(2)}, u32[]{:S(2)}) %collective-permute-start.1) | collective-permute-done | bytes 196640 | tf_op jit(solution)/shard_map/ppermute | solution.py:23
  16.1 1.0 collective-permute-done
  17.2 1.0 fusion.16
  18.5 2.0 %fusion.70 = (bf16[6,8,128,128]{3,2,1,0:T(8,128)(2,1)S(1)}, bf16[6,8,128,128]{3,2,1,0:T(8,128)(2,1)S(1)}, bf16[6,8,128,128]{3,2,1,0:T(8,128)(2,1)S(1)}, bf16[6,8...) fusion(bf16[6,10,130,128]{3,2,1,0:T(8,128)(2,1)S(1)} %fusion.16), kind=kLoop, calls=%fused_computation.110 | loop fusion | bytes 18874368 | tf_op jit(solution)/shard_map/slice | solution.py:58
  21.7 0.6 convolution_add_fusion.14
  23.9 0.6 convolution_add_fusion.10
  25.7 2.6 %fusion.1 = bf16[6,8,128,128]{3,0,2,1:T(8,128)(2,1)S(1)} fusion(f32[6,8,128,128]{3,2,1,0:T(8,128)S(1)} %bitcast.108), kind=kLoop, calls=%fused_computation.23 | loop fusion | flops 3932160 | bytes 4718592 | tf_op jit(solution)/shard_map/convert_element_type | solution.py:143
  28.3 4.1 %collective-permute-start.2 = (bf16[6,1,128,128]{3,0,2,1:T(8,128)(2,1)S(1)}, bf16[6,1,128,128]{3,0,2,1:T(8,128)(2,1)S(1)}, u32[]{:S(2)}, u32[]{:S(2)}) collective-permute-start(bf16[6,1,128,128]{3,0,2,1:T(8,128)(2,1)S(1)} %get-tuple-element.13), channel_id=1, source_target_pairs={{0,1},{1,2},{2,3},{3,4},{4,5},{5,6},{6,7},{8,9},{9,10},{10,11},{11... | collective-permute-start | bytes 589832 | tf_op jit(solution)/shard_map/ppermute | solution.py:21
  32.4 2.3 %collective-permute-start.3 = (bf16[6,1,128,128]{3,0,2,1:T(8,128)(2,1)S(1)}, bf16[6,1,128,128]{3,0,2,1:T(8,128)(2,1)S(1)}, u32[]{:S(2)}, u32[]{:S(2)}) collective-permute-start(bf16[6,1,128,128]{3,0,2,1:T(8,128)(2,1)S(1)} %get-tuple-element.14), channel_id=1, source_target_pairs={{1,0},{2,1},{3,2},{4,3},{5,4},{6,5},{7,6},{9,8},{10,9},{11,10},{12... | collective-permute-start | bytes 589832 | tf_op jit(solution)/shard_map/ppermute | solution.py:23
  34.7 8.5 %collective-permute-done.2 = bf16[6,1,128,128]{3,0,2,1:T(8,128)(2,1)S(1)} collective-permute-done((bf16[6,1,128,128]{3,0,2,1:T(8,128)(2,1)S(1)}, bf16[6,1,128,128]{3,0,2,1:T(8,128)(2,1)S(1)}, u32[]{:S(2)}, u32[]{:S(2)}) %collective-permute-start.2) | collective-permute-done | bytes 196640 | tf_op jit(solution)/shard_map/ppermute | solution.py:21
  43.1 1.8 %collective-permute-done.3 = bf16[6,1,128,128]{3,0,2,1:T(8,128)(2,1)S(1)} collective-permute-done((bf16[6,1,128,128]{3,0,2,1:T(8,128)(2,1)S(1)}, bf16[6,1,128,128]{3,0,2,1:T(8,128)(2,1)S(1)}, u32[]{:S(2)}, u32[]{:S(2)}) %collective-permute-start.3) | collective-permute-done | bytes 196640 | tf_op jit(solution)/shard_map/ppermute | solution.py:23
  45.0 1.2 fusion.11
  46.1 0.8 pad_maximum_fusion
  47.8 3.0 %fusion.68 = (bf16[6,8,128,128]{3,0,2,1:T(8,128)(2,1)S(1)}, bf16[6,8,128,128]{3,0,2,1:T(8,128)(2,1)S(1)}, bf16[6,8,128,128]{3,0,2,1:T(8,128)(2,1)S(1)}, bf16[6,8...) fusion(bf16[6,10,130,128]{3,0,2,1:T(8,128)(2,1)S(1)} %fusion.11), kind=kLoop, calls=%fused_computation.108 | loop fusion | bytes 18874368 | tf_op jit(solution)/shard_map/slice | solution.py:58
  53.1 0.6 copy-done.4
  55.9 1.0 convolution_add_fusion.4
  59.6 22.1 %all_to_all.33 = bf16[6,8,128,128]{3,2,0,1:T(8,128)(2,1)S(1)} all-to-all(bf16[6,8,128,128]{3,2,0,1:T(8,128)(2,1)S(1)} %fusion.6), channel_id=1, replica_groups=mesh['tm'=4,'space'=8] {'tm'}, dimensions={1} | all-to-all | bytes 3145728 | tf_op jit(solution)/shard_map/all_to_all | solution.py:147
  81.7 1.2 copy.55
  82.9 40.0 %temporal.1 = bf16[24,256,128]{2,1,0:T(8,128)(2,1)} custom-call(bf16[24,256,128]{2,1,0:T(8,128)(2,1)} %bitcast.112, f32[1,128]{1,0:T(1,128)} %bitcast.128, bf16[128,384]{1,0:T(8,128)(2,1)} %qkv_ref.1, bf16[128,128]{1,0:T(8,128)(2,1)} %outw_ref.1), custom_call_target="tpu_custom_call" | custom-call | tf_op jit(solution)/shard_map/temporal/pallas_call | solution.py:125
  122.9 23.7 %all_to_all.34 = bf16[24,2,128,128]{3,2,1,0:T(8,128)(2,1)S(1)} all-to-all(bf16[24,2,128,128]{3,2,1,0:T(8,128)(2,1)} %bitcast.113), channel_id=1, replica_groups=mesh['tm'=4,'space'=8] {'tm'}, dimensions={0} | all-to-all | bytes 3145728 | tf_op jit(solution)/shard_map/all_to_all | solution.py:150
  146.6 1.2 copy.56
  (44 shorter events, 13.0 us)
Async XLA Ops:
  0.0 6.9 %copy-start = (bf16[5,2,128,128]{3,2,1,0:T(8,128)(2,1)S(1)}, bf16[5,2,128,128]{3,2,1,0:T(8,128)(2,1)}, u32[]{:S(2)}) copy-start(bf16[5,2,128,128]{3,2,1,0:T(8,128)(2,1)} %param.8) | copy-start | bytes 983044
  1.2 16.0 %copy-start.2 = (bf16[6,8,128,128]{3,2,1,0:T(8,128)(2,1)S(1)}, bf16[6,8,128,128]{3,2,1,0:T(8,128)(2,1)}, u32[]{:S(2)}) copy-start(bf16[6,8,128,128]{3,2,1,0:T(8,128)(2,1)} %param.7) | copy-start | bytes 4718596
  1.3 14.8 %collective-permute-start.1 = (bf16[6,1,128,128]{3,0,2,1:T(8,128)(2,1)S(1)}, bf16[6,1,128,128]{3,0,2,1:T(8,128)(2,1)S(1)}, u32[]{:S(2)}, u32[]{:S(2)}) collective-permute-start(bf16[6,1,128,128]{3,0,2,1:T(8,128)(2,1)S(1)} %copy.59), channel_id=1, source_target_pairs={{1,0},{2,1},{3,2},{4,3},{5,4},{6,5},{7,6},{9,8},{10,9},{11,10},{12... | collective-permute-start | bytes 589832 | tf_op jit(solution)/shard_map/ppermute | solution.py:23
  4.6 12.5 %collective-permute-start = (bf16[6,1,128,128]{3,0,2,1:T(8,128)(2,1)S(1)}, bf16[6,1,128,128]{3,0,2,1:T(8,128)(2,1)S(1)}, u32[]{:S(2)}, u32[]{:S(2)}) collective-permute-start(bf16[6,1,128,128]{3,0,2,1:T(8,128)(2,1)S(1)} %copy.58), channel_id=1, source_target_pairs={{0,1},{1,2},{2,3},{3,4},{4,5},{5,6},{6,7},{8,9},{9,10},{10,11},{11... | collective-permute-start | bytes 589832 | tf_op jit(solution)/shard_map/ppermute | solution.py:21
  18.5 2.0 %copy-start.3 = (bf16[3,3,128,128]{3,2,1,0:T(8,128)(2,1)S(1)}, bf16[3,3,128,128]{3,2,1,0:T(8,128)(2,1)}, u32[]{:S(2)}) copy-start(bf16[3,3,128,128]{3,2,1,0:T(8,128)(2,1)} %param.9) | copy-start | bytes 884740
  28.3 14.9 %collective-permute-start.2 = (bf16[6,1,128,128]{3,0,2,1:T(8,128)(2,1)S(1)}, bf16[6,1,128,128]{3,0,2,1:T(8,128)(2,1)S(1)}, u32[]{:S(2)}, u32[]{:S(2)}) collective-permute-start(bf16[6,1,128,128]{3,0,2,1:T(8,128)(2,1)S(1)} %get-tuple-element.13), channel_id=1, source_target_pairs={{0,1},{1,2},{2,3},{3,4},{4,5},{5,6},{6,7},{8,9},{9,10},{10,11},{11... | collective-permute-start | bytes 589832 | tf_op jit(solution)/shard_map/ppermute | solution.py:21
  32.4 12.5 %collective-permute-start.3 = (bf16[6,1,128,128]{3,0,2,1:T(8,128)(2,1)S(1)}, bf16[6,1,128,128]{3,0,2,1:T(8,128)(2,1)S(1)}, u32[]{:S(2)}, u32[]{:S(2)}) collective-permute-start(bf16[6,1,128,128]{3,0,2,1:T(8,128)(2,1)S(1)} %get-tuple-element.14), channel_id=1, source_target_pairs={{1,0},{2,1},{3,2},{4,3},{5,4},{6,5},{7,6},{9,8},{10,9},{11,10},{12... | collective-permute-start | bytes 589832 | tf_op jit(solution)/shard_map/ppermute | solution.py:23
  52.7 1.0 copy-start.4
  122.9 25.0 %copy-start.1 = (bf16[5,2,128,128]{3,2,1,0:T(8,128)(2,1)S(1)}, bf16[5,2,128,128]{3,2,1,0:T(8,128)(2,1)}, u32[]{:S(2)}) copy-start(bf16[5,2,128,128]{3,2,1,0:T(8,128)(2,1)} %param.8) | copy-start | bytes 983044
where the time goes:
time: 149 us; the launch traced here: 148 us
  blocking collectives  45.8 us (31%)
  Pallas kernels  40 us (27%)
  waiting for transfers between devices  20 us (13%)
  local copies, waits for them, and re-layouts  12.7 us (9%)
  starting transfers between devices  11.8 us (8%)
  matrix products  10.8 us (7%)
  other arithmetic  6.47 us (4%)
    pallas_call x1, Pallas kernels, temporal(): pl.pallas_call(temporal_kernel, out_shape=jax.ShapeDtypeStruct(resid.shap...  40 us
    all_to_all x1, blocking collectives, on_device(): lax.all_to_all(mixed.reshape(layout), 'tm', split_axis=0, concat_axis=1,...  23.7 us
    all_to_all x1, blocking collectives, on_device(): lax.all_to_all(resid, 'tm', split_axis=1, concat_axis=0, tiled=True)  22.1 us
    ppermute x2, waiting for transfers between devices, padded_2(): lax.ppermute(head, axis, [((i + 1) % count, i) for i in range(ends)])  10.6 us
    dot_general x18, matrix products, conv_tile(): jnp.dot(piece, kernel[shift_r, shift_c], preferred_element_type=jnp.float32)  10.4 us
    ppermute x2, waiting for transfers between devices, padded_2(): lax.ppermute(tail, axis, [(i, (i + 1) % count) for i in range(ends)])  9.45 us
    slice x10, local copies, waits for them, and re-layouts, conv_tile(): padded[:, shift_r:shift_r + rows, shift_c:shift_c + width]  8.11 us
    ppermute x2, starting transfers between devices, padded_2(): lax.ppermute(tail, axis, [(i, (i + 1) % count) for i in range(ends)])  6.34 us
  transfers between devices with their start and end apart: 4, of which 4 were waited for; matrix products, arithmetic and copies ran while one was open for 0% of the time, Pallas kernels for 0%

commit v1 on v0

v1 whole, which is shorter than its diff:
```python
import functools

import jax
import jax.numpy as jnp
from jax import lax
from jax.experimental import pallas as pl
from jax.experimental.pallas import tpu as pltpu
from jax.sharding import PartitionSpec as P

HEADS = 8
FRAMES = 24
COARSE = 5


def interp_matrix(times):
    scaled = times * (COARSE - 1)
    lower = scaled // (FRAMES - 1)
    upper = jnp.minimum(lower + 1, COARSE - 1)
    frac = (scaled - lower * (FRAMES - 1)).astype(jnp.float32) / float(FRAMES - 1)
    levels = jnp.arange(COARSE, dtype=jnp.int32)
    low_hot = (levels[None, :] == lower[:, None]).astype(jnp.float32)
    up_hot = (levels[None, :] == upper[:, None]).astype(jnp.float32)
    return (1.0 - frac)[:, None] * low_hot + frac[:, None] * up_hot


def attend_pixels(x, qkv_weight, norm_gain, out_weight, mask, heads_of):
    nframes, group, chans = x.shape
    rows = nframes * group
    head_dim = chans // HEADS
    x = x.reshape(rows, chans)
    mean_sq = jnp.mean(x * x, axis=-1, keepdims=True)
    normed = (x * lax.rsqrt(mean_sq + 1e-06) * norm_gain).astype(jnp.bfloat16)
    qkv = jnp.dot(normed, qkv_weight, preferred_element_type=jnp.float32).astype(jnp.bfloat16)
    query = qkv[:, :chans] * jnp.bfloat16(1.0 / head_dim**0.5)
    key_part = qkv[:, chans : 2 * chans]
    value = qkv[:, 2 * chans :]
    with_ones = jnp.concatenate([value, jnp.ones_like(value)], axis=1)
    num = jnp.zeros((rows, chans), jnp.float32)
    den = jnp.ones((rows, chans), jnp.float32)
    for head in range(HEADS):
        own = heads_of == head
        picked = jnp.where(own, query, jnp.zeros_like(query))
        scores = lax.dot_general(
            picked, key_part, (((1,), (1,)), ((), ())), preferred_element_type=jnp.float32
        )
        scores = scores + mask
        top = jnp.max(scores, axis=-1, keepdims=True)
        expd = jnp.exp(scores - top).astype(jnp.bfloat16)
        both = jnp.dot(expd, with_ones, preferred_element_type=jnp.float32)
        num = jnp.where(own, both[:, :chans], num)
        den = jnp.where(own, both[:, chans:], den)
    attended = (num / den).astype(jnp.bfloat16)
    out = x + jnp.dot(attended, out_weight, preferred_element_type=jnp.float32)
    return out.reshape(nframes, group, chans)


MESH = pl.DeviceIdType.MESH
STEP = 16
CHUNK = 4


def conv_taps(taps, weight, width):
    cells = jnp.concatenate(taps, axis=1)
    rows = cells.shape[0]
    chans = weight.shape[1] // 3
    wide = jnp.dot(cells, weight, preferred_element_type=jnp.float32)
    col = lax.rem(lax.broadcasted_iota(jnp.int32, (rows, chans), 0), width)
    left = jnp.where(col == 0, 0.0, pltpu.roll(wide[:, :chans], 1, 0))
    right = jnp.where(col == width - 1, 0.0, pltpu.roll(wide[:, 2 * chans :], rows - 1, 0))
    return wide[:, chans : 2 * chans] + left + right


def block_kernel(
    peers, spaces,
    x_ref, strips_ref, w1_ref, w2_ref, gain_ref, qkv_ref, outw_ref, o_ref,
    xpad, hpad, sbuf, rbuf, abuf, wcat, mask_ref,
    local_sem, halo_send, halo_recv, there_send, there_recv, back_send, back_recv, own_sem,
):
    nloc, rows, width, chans = x_ref.shape
    nframes = nloc * peers
    share = rows // peers
    me = lax.axis_index("tm")
    place = lax.axis_index("space")
    last = spaces - 1

    def peer_of(k):
        chip = lax.rem(me // 2 + k // 2, peers // 2)
        return chip * 2 + lax.rem(me + k % 2, 2)

    own_rows = pltpu.make_async_copy(x_ref, xpad.at[:, pl.ds(2, rows)], local_sem)
    own_rows.start()

    barrier = pltpu.get_barrier_semaphore()
    for k in range(1, peers):
        pl.semaphore_signal(barrier, inc=1, device_id={"tm": peer_of(k)}, device_id_type=MESH)

    @pl.when(place > 0)
    def _():
        pl.semaphore_signal(barrier, inc=1, device_id={"space": place - 1}, device_id_type=MESH)

    @pl.when(place < last)
    def _():
        pl.semaphore_signal(barrier, inc=1, device_id={"space": place + 1}, device_id_type=MESH)

    beside = jnp.where(place > 0, 1, 0) + jnp.where(place < last, 1, 0)
    pl.semaphore_wait(barrier, peers - 1 + beside)

    up = pltpu.make_async_remote_copy(
        x_ref.at[:, pl.ds(0, 2)], xpad.at[:, pl.ds(rows + 2, 2)],
        halo_send.at[0], halo_recv.at[0], device_id={"space": place - 1}, device_id_type=MESH,
    )
    down = pltpu.make_async_remote_copy(
        x_ref.at[:, pl.ds(rows - 2, 2)], xpad.at[:, pl.ds(0, 2)],
        halo_send.at[1], halo_recv.at[1], device_id={"space": place + 1}, device_id_type=MESH,
    )

    @pl.when(place > 0)
    def _():
        up.start()

    @pl.when(place < last)
    def _():
        down.start()

    for which, ref in enumerate((w1_ref, w2_ref)):
        for dy in range(3):
            for dx in range(3):
                wcat[which, dy * chans : (dy + 1) * chans, dx * chans : (dx + 1) * chans] = ref[dy, dx]
    group = nframes * 8
    row_id = lax.broadcasted_iota(jnp.int32, (group, group), 0)
    col_id = lax.broadcasted_iota(jnp.int32, (group, group), 1)
    mask_ref[...] = jnp.where(lax.rem(row_id, 8) == lax.rem(col_id, 8), 0.0, -1e30)
    heads_of = lax.broadcasted_iota(jnp.int32, (group, chans), 1) // (chans // HEADS)

    def hidden_rows(frame, row):
        taps = [xpad[frame, row + dy : row + dy + 2].reshape(2 * width, chans) for dy in range(3)]
        first = conv_taps(taps, wcat[0], width)
        act = (first / (1.0 + jnp.exp(-first))).astype(jnp.bfloat16)
        hpad[frame, row : row + 2] = act.reshape(2, width, chans)

    own_rows.wait()

    def interior(frame, carry):
        for row in range(2, rows, 2):
            hidden_rows(frame, row)
        return carry

    lax.fori_loop(0, nloc, interior, 0)

    @pl.when(place > 0)
    def _():
        down.wait_recv()

    @pl.when(place == 0)
    def _():
        xpad[:, 0] = strips_ref[:, 0]
        xpad[:, 1] = strips_ref[:, 0]

    @pl.when(place < last)
    def _():
        up.wait_recv()

    @pl.when(place == last)
    def _():
        xpad[:, rows + 2] = strips_ref[:, 1]
        xpad[:, rows + 3] = strips_ref[:, 1]

    def border(frame, carry):
        hidden_rows(frame, 0)
        hidden_rows(frame, rows)
        return carry

    lax.fori_loop(0, nloc, border, 0)

    @pl.when(place == 0)
    def _():
        hpad[:, 0] = strips_ref[:, 0]

    @pl.when(place == last)
    def _():
        hpad[:, rows + 1] = strips_ref[:, 1]

    def there(h, k):
        row = peer_of(k) * share + h
        return pltpu.make_async_remote_copy(
            sbuf.at[row], rbuf.at[h, pl.ds(me * nloc, nloc)],
            there_send.at[h, k], there_recv.at[h, k],
            device_id={"tm": peer_of(k)}, device_id_type=MESH,
        )

    pending = None
    for h in range(share):
        for k in list(range(2, peers)) + [1, 0]:
            row = peer_of(k) * share + h

            def second_rows(i, carry, row=row, h=h, k=k):
                frames = pl.ds(i * 2, 2)
                taps = [hpad[frames, row + dy].reshape(2 * width, chans) for dy in range(3)]
                second = conv_taps(taps, wcat[1], width)
                resid = xpad[frames, row + 2].astype(jnp.float32) + second.reshape(2, width, chans)
                if k == 0:
                    rbuf[h, pl.ds(me * nloc + i * 2, 2)] = resid.astype(jnp.bfloat16)
                else:
                    sbuf[row, frames] = resid.astype(jnp.bfloat16)
                return carry

            lax.fori_loop(0, nloc // 2, second_rows, 0)
            if pending is not None:
                there(*pending).start()
            pending = (h, k) if k else None

    per_row = width // STEP
    chunks_per_row = per_row // CHUNK
    total = share * per_row

    def chunk_cols(c):
        h = c // chunks_per_row
        start = pl.multiple_of(lax.rem(c, chunks_per_row) * (CHUNK * STEP), CHUNK * STEP)
        return h, pl.ds(start, CHUNK * STEP)

    def back(c, k):
        h, cols = chunk_cols(c)
        return pltpu.make_async_remote_copy(
            abuf.at[h, pl.ds(peer_of(k) * nloc, nloc), cols],
            o_ref.at[:, me * share + h, cols],
            back_send.at[c, k], back_recv.at[c, k],
            device_id={"tm": peer_of(k)}, device_id_type=MESH,
        )

    def keep(c):
        h, cols = chunk_cols(c)
        return pltpu.make_async_copy(
            abuf.at[h, pl.ds(me * nloc, nloc), cols], o_ref.at[:, me * share + h, cols], own_sem.at[c]
        )

    def send_back(c):
        for k in list(range(2, peers)) + [1]:
            back(c, k).start()
        keep(c).start()

    def step(s, carry):
        h = s // per_row
        inner = lax.rem(s, per_row)

        @pl.when(inner == 0)
        def _():
            for k in range(1, peers):
                there(h, k).wait_recv()

        cols = pl.ds(pl.multiple_of(inner * STEP, STEP), STEP)
        x = rbuf[h, :, cols, :].astype(jnp.float32)
        halves = [
            attend_pixels(
                x[:, j * 8 : j * 8 + 8], qkv_ref[...], gain_ref[...], outw_ref[...],
                mask_ref[...], heads_of,
            )
            for j in range(STEP // 8)
        ]
        abuf[h, :, cols, :] = jnp.concatenate(halves, axis=1).astype(jnp.bfloat16)

        @pl.when(lax.rem(s, CHUNK) == CHUNK - 1)
        def _():
            send_back(s // CHUNK)

        return carry

    lax.fori_loop(0, total, step, 0)

    @pl.when(place > 0)
    def _():
        up.wait_send()

    @pl.when(place < last)
    def _():
        down.wait_send()

    for h in range(share):
        for k in range(1, peers):
            there(h, k).wait_send()

    def drain(c, carry):
        for k in range(1, peers):
            back(c, k).wait()
        keep(c).wait()
        return carry

    lax.fori_loop(0, total // CHUNK, drain, 0)


def on_device(frames_in, boundary, conv_first, conv_second, norm_gain, qkv_weight, out_weight):
    nloc, rows, width, chans = frames_in.shape
    peers = lax.axis_size("tm")
    spaces = lax.axis_size("space")
    nframes = nloc * peers
    share = rows // peers
    chunks = share * width // (STEP * CHUNK)
    times = lax.axis_index("tm") * nloc + jnp.arange(nloc, dtype=jnp.int32)
    weights = interp_matrix(times)
    strips = jnp.einsum("tk,kscx->tscx", weights, boundary.astype(jnp.float32)).astype(jnp.bfloat16)
    vmem = pl.BlockSpec(memory_space=pltpu.VMEM)
    hbm = pl.BlockSpec(memory_space=pl.ANY)
    bf16 = jnp.bfloat16
    dma = pltpu.SemaphoreType.DMA
    return pl.pallas_call(
        functools.partial(block_kernel, peers, spaces),
        out_shape=jax.ShapeDtypeStruct(frames_in.shape, frames_in.dtype),
        in_specs=[hbm] + [vmem] * 6,
        out_specs=hbm,
        scratch_shapes=[
            pltpu.VMEM((nloc, rows + 4, width, chans), bf16),
            pltpu.VMEM((nloc, rows + 2, width, chans), bf16),
            pltpu.VMEM((rows, nloc, width, chans), bf16),
            pltpu.VMEM((share, nframes, width, chans), bf16),
            pltpu.VMEM((share, nframes, width, chans), bf16),
            pltpu.VMEM((2, 3 * chans, 3 * chans), bf16),
            pltpu.VMEM((nframes * 8, nframes * 8), jnp.float32),
            dma, dma((2,)), dma((2,)), dma((share, peers)), dma((share, peers)),
            dma((chunks, peers)), dma((chunks, peers)), dma((chunks,)),
        ],
        compiler_params=pltpu.CompilerParams(
            collective_id=0, has_side_effects=True, vmem_limit_bytes=48 * 1024 * 1024
        ),
        name="denoise",
    )(frames_in, strips, conv_first, conv_second, norm_gain.reshape(1, chans), qkv_weight, out_weight)


def solution(mesh):
    placed = (P("tm", "space", None, None), P(), P(), P(), P(), P(), P())
    return jax.shard_map(
        on_device,
        mesh=mesh,
        in_specs=placed,
        out_specs=P("tm", "space", None, None),
        check_vma=False,
    )
```

time: 149 us -> 84.5 us (0.57)
  blocking collectives: 45.8 us -> 0 us
  Pallas kernels: 40 us -> 79.5 us
  waiting for transfers between devices: 20 us -> 0 us
  starting transfers between devices: 11.8 us -> 0 us
  matrix products: 10.8 us -> 0.36 us
  local copies, waits for them, and re-layouts: 12.7 us -> 4.07 us
  other arithmetic: 6.47 us -> 0.04 us
    all_to_all x2 -> x0, blocking collectives: 45.8 us -> none  [the longest x1 23.7 us: on_device(): lax.all_to_all(mixed.reshape(layout), 'tm', split_axis=0, concat_axis=1,...]
    pallas_call x1, Pallas kernels: 40 us -> 79.5 us  [on_device(): pl.pallas_call(functools.partial(block_kernel, peers, spaces), out_shape=...]
    ppermute x4 -> x0, waiting for transfers between devices: 20 us -> none  [the longest x2 10.6 us: padded_2(): lax.ppermute(head, axis, [((i + 1) % count, i) for i in range(ends)])]
    ppermute x4 -> x0, starting transfers between devices: 11.8 us -> none  [the longest x2 6.34 us: padded_2(): lax.ppermute(tail, axis, [(i, (i + 1) % count) for i in range(ends)])]
    dot_general x18 -> x0, matrix products: 10.4 us -> none  [conv_tile(): jnp.dot(piece, kernel[shift_r, shift_c], preferred_element_type=jnp.float32)]
    slice x12 -> x0, local copies, waits for them, and re-layouts: 9.24 us -> none  [the longest x10 8.11 us: conv_tile(): padded[:, shift_r:shift_r + rows, shift_c:shift_c + width]]
    concatenate x4 -> x0, other arithmetic: 3.24 us -> none  [fix_edges(): rows = jnp.concatenate([top_row, padded[:, 1:-1], bottom_row], axis=1)]
    unnamed x12 -> x15, local copies, waits for them, and re-layouts: 0.88 us -> 4.01 us
  transfers between devices with their start and end apart: 4 -> 0, of which waited for: 4 -> 0; matrix products, arithmetic and copies ran while one was open for 0% -> 0% of each run, Pallas kernels for 0% -> 0%
where the time goes in v1:
time: 84.5 us; the launch traced here: 84.1 us
  Pallas kernels  79.5 us (94%)
  local copies, waits for them, and re-layouts  4.07 us (5%)
    pallas_call x1, Pallas kernels, on_device(): pl.pallas_call(functools.partial(block_kernel, peers, spaces), out_shape=...  79.5 us
    unnamed x15, local copies, waits for them, and re-layouts  4.01 us

profile of v1, /device:TPU:17, one launch (start us, length us, event | category | flops | bytes accessed | tf_op | source)
XLA Modules:
  0.0 84.1 jit_solution(989808489300970097)
XLA Ops:
  0.0 0.0 copy-start
  0.0 0.0 copy-start.4
  0.0 0.0 copy-start.6
  0.0 0.0 copy-start.2
  0.0 0.0 copy-start.1
  0.1 0.9 %copy-done = bf16[5,2,128,128]{3,2,1,0:T(8,128)(2,1)S(1)} copy-done((bf16[5,2,128,128]{3,2,1,0:T(8,128)(2,1)S(1)}, bf16[5,2,128,128]{3,2,1,0:T(8,128)(2,1)}, u32[]{:S(2)}) %copy-start) | copy-done | bytes 327704
  1.0 0.4 fusion
  1.3 0.1 copy.14.strips_ref
  1.4 0.0 copy-done.4
  1.4 0.0 copy-done.6
  1.4 0.0 copy-done.2
  1.4 0.2 copy-done.1
  1.7 0.0 copy-start.3
  1.7 1.0 %copy-done.3 = bf16[3,3,128,128]{3,2,1,0:T(8,128)(2,1)S(1)} copy-done((bf16[3,3,128,128]{3,2,1,0:T(8,128)(2,1)S(1)}, bf16[3,3,128,128]{3,2,1,0:T(8,128)(2,1)}, u32[]{:S(2)}) %copy-start.3) | copy-done | bytes 294936
  2.6 0.0 copy-start.5
  2.6 0.8 copy-done.5
  3.4 79.5 %denoise.1 = bf16[6,8,128,128]{3,2,1,0:T(8,128)(2,1)S(1)} custom-call(bf16[6,8,128,128]{3,2,1,0:T(8,128)(2,1)S(1)} %copy-done.1, bf16[6,2,128,128]{3,2,1,0:T(8,128)(2,1)S(1)} %copy.14.strips_ref, bf16[3,3,128,128]{3,2,1,0:T(8,128)(2,1)S(1)} %copy-done.2, bf16[3,3,128,128]{3,2,1,0:T(8,128)(2,1)S(1)} %copy-done.3, f32[1,128]{1,0:T(1,128)S(1)} %bitcast.6, ...), custom_call_target="tpu_custom_call" | custom-call | tf_op jit(solution)/shard_map/denoise/pallas_call | solution.py:304
  82.9 1.1 %copy.16 = bf16[6,8,128,128]{3,2,1,0:T(8,128)(2,1)} copy(bf16[6,8,128,128]{3,2,1,0:T(8,128)(2,1)S(1)} %denoise.1) | data formatting | bytes 3145728
  (2 shorter events, 0.0 us)
Async XLA Ops:
  0.0 1.0 %copy-start = (bf16[5,2,128,128]{3,2,1,0:T(8,128)(2,1)S(1)}, bf16[5,2,128,128]{3,2,1,0:T(8,128)(2,1)}, u32[]{:S(2)}) copy-start(bf16[5,2,128,128]{3,2,1,0:T(8,128)(2,1)} %param.8) | copy-start | bytes 983044
  0.0 1.4 %copy-start.4 = (bf16[128,384]{1,0:T(8,128)(2,1)S(1)}, bf16[128,384]{1,0:T(8,128)(2,1)}, u32[]{:S(2)}) copy-start(bf16[128,384]{1,0:T(8,128)(2,1)} %qkv_ref.1) | copy-start | bytes 294916
  0.0 1.4 %copy-start.6 = (f32[128]{0:T(128)S(1)}, f32[128]{0:T(128)}, u32[]{:S(2)}) copy-start(f32[128]{0:T(128)} %param.11) | copy-start | bytes 1540
  0.0 1.4 %copy-start.2 = (bf16[3,3,128,128]{3,2,1,0:T(8,128)(2,1)S(1)}, bf16[3,3,128,128]{3,2,1,0:T(8,128)(2,1)}, u32[]{:S(2)}) copy-start(bf16[3,3,128,128]{3,2,1,0:T(8,128)(2,1)} %w1_ref.1) | copy-start | bytes 884740
  0.0 1.7 %copy-start.1 = (bf16[6,8,128,128]{3,2,1,0:T(8,128)(2,1)S(1)}, bf16[6,8,128,128]{3,2,1,0:T(8,128)(2,1)}, u32[]{:S(2)}) copy-start(bf16[6,8,128,128]{3,2,1,0:T(8,128)(2,1)} %x_ref.1) | copy-start | bytes 4718596
  1.7 1.0 %copy-start.3 = (bf16[3,3,128,128]{3,2,1,0:T(8,128)(2,1)S(1)}, bf16[3,3,128,128]{3,2,1,0:T(8,128)(2,1)}, u32[]{:S(2)}) copy-start(bf16[3,3,128,128]{3,2,1,0:T(8,128)(2,1)} %w2_ref.1) | copy-start | bytes 884740
  2.6 0.8 copy-start.5

commit v2 on v1

--- a/solution.py
+++ b/solution.py
@@ -23,40 +23,47 @@
     return (1.0 - frac)[:, None] * low_hot + frac[:, None] * up_hot
 
 
-def attend_pixels(x, qkv_weight, norm_gain, out_weight, mask, heads_of):
-    nframes, group, chans = x.shape
-    rows = nframes * group
+def attend_block(x, qkv_weight, norm_gain, out_weight, mask, heads_of):
+    nframes, cells, chans = x.shape
+    rows = nframes * 8
     head_dim = chans // HEADS
-    x = x.reshape(rows, chans)
+    parts = [x[:, j : j + 8].reshape(rows, chans) for j in range(0, cells, 8)]
+    x = jnp.concatenate(parts, axis=0)
     mean_sq = jnp.mean(x * x, axis=-1, keepdims=True)
     normed = (x * lax.rsqrt(mean_sq + 1e-06) * norm_gain).astype(jnp.bfloat16)
     qkv = jnp.dot(normed, qkv_weight, preferred_element_type=jnp.float32).astype(jnp.bfloat16)
-    query = qkv[:, :chans] * jnp.bfloat16(1.0 / head_dim**0.5)
-    key_part = qkv[:, chans : 2 * chans]
-    value = qkv[:, 2 * chans :]
-    with_ones = jnp.concatenate([value, jnp.ones_like(value)], axis=1)
-    num = jnp.zeros((rows, chans), jnp.float32)
-    den = jnp.ones((rows, chans), jnp.float32)
-    for head in range(HEADS):
-        own = heads_of == head
-        picked = jnp.where(own, query, jnp.zeros_like(query))
+    outs = []
+    for g in range(len(parts)):
+        mine = qkv[g * rows : (g + 1) * rows]
+        query = mine[:, :chans] * jnp.bfloat16(1.0 / head_dim**0.5)
+        key_part = mine[:, chans : 2 * chans]
+        value = mine[:, 2 * chans :]
+        with_ones = jnp.concatenate([value, jnp.ones_like(value)], axis=1)
+        picked = jnp.concatenate(
+            [jnp.where(heads_of == h, query, jnp.zeros_like(query)) for h in range(HEADS)], axis=0
+        )
         scores = lax.dot_general(
             picked, key_part, (((1,), (1,)), ((), ())), preferred_element_type=jnp.float32
         )
-        scores = scores + mask
+        scores = (scores.reshape(HEADS, rows, rows) + mask).reshape(HEADS * rows, rows)
         top = jnp.max(scores, axis=-1, keepdims=True)
-        expd = jnp.exp(scores - top).astype(jnp.bfloat16)
+        expd = jnp.exp((scores - top).astype(jnp.bfloat16))
         both = jnp.dot(expd, with_ones, preferred_element_type=jnp.float32)
-        num = jnp.where(own, both[:, :chans], num)
-        den = jnp.where(own, both[:, chans:], den)
-    attended = (num / den).astype(jnp.bfloat16)
+        num, den = both[:rows, :chans], both[:rows, chans:]
+        for h in range(1, HEADS):
+            piece = both[h * rows : (h + 1) * rows]
+            own = heads_of == h
+            num = jnp.where(own, piece[:, :chans], num)
+            den = jnp.where(own, piece[:, chans:], den)
+        outs.append((num / den).astype(jnp.bfloat16))
+    attended = jnp.concatenate(outs, axis=0)
     out = x + jnp.dot(attended, out_weight, preferred_element_type=jnp.float32)
-    return out.reshape(nframes, group, chans)
+    return jnp.concatenate([out[g * rows : (g + 1) * rows].reshape(nframes, 8, chans) for g in range(len(parts))], axis=1)
 
 
 MESH = pl.DeviceIdType.MESH
-STEP = 16
-CHUNK = 4
+STEP = 64
+CHUNK = 1
 
 
 def conv_taps(taps, weight, width):
@@ -193,18 +200,13 @@
         for k in list(range(2, peers)) + [1, 0]:
             row = peer_of(k) * share + h
 
-            def second_rows(i, carry, row=row, h=h, k=k):
-                frames = pl.ds(i * 2, 2)
-                taps = [hpad[frames, row + dy].reshape(2 * width, chans) for dy in range(3)]
-                second = conv_taps(taps, wcat[1], width)
-                resid = xpad[frames, row + 2].astype(jnp.float32) + second.reshape(2, width, chans)
-                if k == 0:
-                    rbuf[h, pl.ds(me * nloc + i * 2, 2)] = resid.astype(jnp.bfloat16)
-                else:
-                    sbuf[row, frames] = resid.astype(jnp.bfloat16)
-                return carry
-
-            lax.fori_loop(0, nloc // 2, second_rows, 0)
+            taps = [hpad[:, row + dy].reshape(nloc * width, chans) for dy in range(3)]
+            second = conv_taps(taps, wcat[1], width).reshape(nloc, width, chans)
+            resid = (xpad[:, row + 2].astype(jnp.float32) + second).astype(jnp.bfloat16)
+            if k == 0:
+                rbuf[h, pl.ds(me * nloc, nloc)] = resid
+            else:
+                sbuf[row] = resid
             if pending is not None:
                 there(*pending).start()
             pending = (h, k) if k else None
@@ -249,14 +251,10 @@
 
         cols = pl.ds(pl.multiple_of(inner * STEP, STEP), STEP)
         x = rbuf[h, :, cols, :].astype(jnp.float32)
-        halves = [
-            attend_pixels(
-                x[:, j * 8 : j * 8 + 8], qkv_ref[...], gain_ref[...], outw_ref[...],
-                mask_ref[...], heads_of,
-            )
-            for j in range(STEP // 8)
-        ]
-        abuf[h, :, cols, :] = jnp.concatenate(halves, axis=1).astype(jnp.bfloat16)
+        mixed = attend_block(
+            x, qkv_ref[...], gain_ref[...], outw_ref[...], mask_ref[...], heads_of
+        )
+        abuf[h, :, cols, :] = mixed.astype(jnp.bfloat16)
 
         @pl.when(lax.rem(s, CHUNK) == CHUNK - 1)
         def _():

time: 84.5 us -> 65.1 us (0.77)
  Pallas kernels: 79.5 us -> 60.3 us
    pallas_call x1, Pallas kernels: 79.5 us -> 60.3 us  [on_device(): pl.pallas_call(functools.partial(block_kernel, peers, spaces), out_shape=...]
where the time goes in v2:
time: 65.1 us; the launch traced here: 64.9 us
  Pallas kernels  60.3 us (93%)
  local copies, waits for them, and re-layouts  4.07 us (6%)
    pallas_call x1, Pallas kernels, on_device(): pl.pallas_call(functools.partial(block_kernel, peers, spaces), out_shape=...  60.3 us
    unnamed x15, local copies, waits for them, and re-layouts  4.01 us

profile of v2, /device:TPU:17, one launch (start us, length us, event | category | flops | bytes accessed | tf_op | source)
XLA Modules:
  0.0 64.9 jit_solution(702681553871919864)
XLA Ops:
  0.0 0.0 copy-start
  0.0 0.0 copy-start.4
  0.0 0.0 copy-start.6
  0.0 0.0 copy-start.2
  0.0 0.0 copy-start.1
  0.1 0.9 %copy-done = bf16[5,2,128,128]{3,2,1,0:T(8,128)(2,1)S(1)} copy-done((bf16[5,2,128,128]{3,2,1,0:T(8,128)(2,1)S(1)}, bf16[5,2,128,128]{3,2,1,0:T(8,128)(2,1)}, u32[]{:S(2)}) %copy-start) | copy-done | bytes 327704
  1.0 0.4 fusion
  1.3 0.1 copy.14.strips_ref
  1.4 0.0 copy-done.4
  1.4 0.0 copy-done.6
  1.4 0.0 copy-done.2
  1.4 0.2 copy-done.1
  1.7 0.0 copy-start.3
  1.7 1.0 %copy-done.3 = bf16[3,3,128,128]{3,2,1,0:T(8,128)(2,1)S(1)} copy-done((bf16[3,3,128,128]{3,2,1,0:T(8,128)(2,1)S(1)}, bf16[3,3,128,128]{3,2,1,0:T(8,128)(2,1)}, u32[]{:S(2)}) %copy-start.3) | copy-done | bytes 294936
  2.6 0.0 copy-start.5
  2.6 0.8 %copy-done.5 = bf16[128,128]{1,0:T(8,128)(2,1)S(1)} copy-done((bf16[128,128]{1,0:T(8,128)(2,1)S(1)}, bf16[128,128]{1,0:T(8,128)(2,1)}, u32[]{:S(2)}) %copy-start.5) | copy-done | bytes 32792
  3.4 60.3 %denoise.1 = bf16[6,8,128,128]{3,2,1,0:T(8,128)(2,1)S(1)} custom-call(bf16[6,8,128,128]{3,2,1,0:T(8,128)(2,1)S(1)} %copy-done.1, bf16[6,2,128,128]{3,2,1,0:T(8,128)(2,1)S(1)} %copy.14.strips_ref, bf16[3,3,128,128]{3,2,1,0:T(8,128)(2,1)S(1)} %copy-done.2, bf16[3,3,128,128]{3,2,1,0:T(8,128)(2,1)S(1)} %copy-done.3, f32[1,128]{1,0:T(1,128)S(1)} %bitcast.6, ...), custom_call_target="tpu_custom_call" | custom-call | tf_op jit(solution)/shard_map/denoise/pallas_call | solution.py:302
  63.7 1.1 %copy.16 = bf16[6,8,128,128]{3,2,1,0:T(8,128)(2,1)} copy(bf16[6,8,128,128]{3,2,1,0:T(8,128)(2,1)S(1)} %denoise.1) | data formatting | bytes 3145728
  (2 shorter events, 0.0 us)
Async XLA Ops:
  0.0 1.0 %copy-start = (bf16[5,2,128,128]{3,2,1,0:T(8,128)(2,1)S(1)}, bf16[5,2,128,128]{3,2,1,0:T(8,128)(2,1)}, u32[]{:S(2)}) copy-start(bf16[5,2,128,128]{3,2,1,0:T(8,128)(2,1)} %param.8) | copy-start | bytes 983044
  0.0 1.4 %copy-start.4 = (bf16[128,384]{1,0:T(8,128)(2,1)S(1)}, bf16[128,384]{1,0:T(8,128)(2,1)}, u32[]{:S(2)}) copy-start(bf16[128,384]{1,0:T(8,128)(2,1)} %qkv_ref.1) | copy-start | bytes 294916
  0.0 1.4 %copy-start.6 = (f32[128]{0:T(128)S(1)}, f32[128]{0:T(128)}, u32[]{:S(2)}) copy-start(f32[128]{0:T(128)} %param.11) | copy-start | bytes 1540
  0.0 1.4 %copy-start.2 = (bf16[3,3,128,128]{3,2,1,0:T(8,128)(2,1)S(1)}, bf16[3,3,128,128]{3,2,1,0:T(8,128)(2,1)}, u32[]{:S(2)}) copy-start(bf16[3,3,128,128]{3,2,1,0:T(8,128)(2,1)} %w1_ref.1) | copy-start | bytes 884740
  0.0 1.7 %copy-start.1 = (bf16[6,8,128,128]{3,2,1,0:T(8,128)(2,1)S(1)}, bf16[6,8,128,128]{3,2,1,0:T(8,128)(2,1)}, u32[]{:S(2)}) copy-start(bf16[6,8,128,128]{3,2,1,0:T(8,128)(2,1)} %x_ref.1) | copy-start | bytes 4718596
  1.7 1.0 %copy-start.3 = (bf16[3,3,128,128]{3,2,1,0:T(8,128)(2,1)S(1)}, bf16[3,3,128,128]{3,2,1,0:T(8,128)(2,1)}, u32[]{:S(2)}) copy-start(bf16[3,3,128,128]{3,2,1,0:T(8,128)(2,1)} %w2_ref.1) | copy-start | bytes 884740
  2.6 0.8 %copy-start.5 = (bf16[128,128]{1,0:T(8,128)(2,1)S(1)}, bf16[128,128]{1,0:T(8,128)(2,1)}, u32[]{:S(2)}) copy-start(bf16[128,128]{1,0:T(8,128)(2,1)} %outw_ref.1) | copy-start | bytes 98308
